TPU v7x, 256 devices: a whole 4x4x8 slice. The times are simulated.
256 devices in a mesh: row: 8 (over z_lo, x), col: 32 (over z_hi, y, core).
Axes of the slice: x: 4, y: 4, z: 8 (z_hi: 4, z_lo: 2; z = z_hi * 2 + z_lo), core: 2. Of those that a mesh axis runs over, the one named last changes fastest.
Arguments:
- image_feats: bfloat16 [3, 56, 224, 1024], P(None, 'row', 'col'), may hold values from -80 to 80
- norm_gain: float32 [1024], replicated, may hold values from 0.5 to 1.5
- w_qkv: bfloat16 [1024, 1536], replicated, may hold values from -0.1875 to 0.1875
- rel_bias: float32 [8, 13, 13], replicated, may hold values from -5 to 355
- w_proj: bfloat16 [512, 1024], replicated, may hold values from -0.25 to 0.25
- out_grad: bfloat16 [3, 56, 224, 1024], P(None, 'row', 'col'), may hold values from -6 to 6
Outputs:
- layer_out: bfloat16 [3, 56, 224, 1024], P(None, 'row', 'col')
- feats_grad: bfloat16 [3, 56, 224, 1024], P(None, 'row', 'col')
- qkv_grad: bfloat16 [1024, 1536], replicated
- proj_grad: bfloat16 [512, 1024], replicated
- gain_grad: float32 [1024], replicated
- bias_grad: float32 [8, 13, 13], replicated
All inputs are finite; a program needn't handle non-finite values.
Results may differ from a plain program's by a relative error of at most 0.017.
Values may be sent and summed in bfloat16 or wider, within the bound.
No kernel may reach another device: no remote copies, remote signals or barrier semaphores. Data moves between devices by JAX's collectives and lax.ppermute only.
A program may use at most 128 MiB of HBM per device.

v0:
```python
import jax
import jax.numpy as jnp
from jax import lax
from jax.sharding import PartitionSpec as P

WIN = 7
norm_eps = 1e-05
highest = lax.Precision.HIGHEST


def shifted(value, axis, steps):
    count = lax.axis_size(axis)
    leading, last = (max(0, -steps), min(count, count - steps))
    return lax.ppermute(value, axis, [(source, source + steps) for source in range(leading, last)])


def with_halo(block, sides, width):
    for axis, dim in sides:
        count = lax.axis_size(axis)
        forward = [(i, i + 1) for i in range(count - 1)]
        backward = [(target, source) for source, target in forward]
        low = lax.ppermute(
            lax.slice_in_dim(block, block.shape[dim] - width, None, axis=dim), axis, forward
        )
        high = lax.ppermute(lax.slice_in_dim(block, 0, width, axis=dim), axis, backward)
        block = jnp.concatenate([low, block, high], axis=dim)
    return block


def window_start(extent, length, anchor):
    position = anchor + jnp.arange(length, dtype=jnp.int32)
    return jnp.clip(position - WIN // 2, 0, extent - WIN)


def return_rims(grad_pad, half_win):
    top_rim = grad_pad[:, :half_win]
    bottom_rim = grad_pad[:, -half_win:]
    from_below = shifted(top_rim.astype(jnp.bfloat16), "row", -1).astype(top_rim.dtype)
    from_above = shifted(bottom_rim.astype(jnp.bfloat16), "row", 1).astype(bottom_rim.dtype)
    middle = grad_pad[:, half_win:-half_win]
    middle = middle.at[:, :half_win].add(from_above)
    middle = middle.at[:, -half_win:].add(from_below)
    left_rim = middle[:, :, :half_win]
    right_rim = middle[:, :, -half_win:]
    from_right = shifted(left_rim.astype(jnp.bfloat16), "col", -1).astype(left_rim.dtype)
    from_left = shifted(right_rim.astype(jnp.bfloat16), "col", 1).astype(right_rim.dtype)
    inner_part = middle[:, :, half_win:-half_win]
    inner_part = inner_part.at[:, :, :half_win].add(from_left)
    inner_part = inner_part.at[:, :, -half_win:].add(from_right)
    return inner_part


def body(image_feats, norm_gain, w_qkv, rel_bias, w_proj, out_grad):
    tile_count, row_count, col_count, model_dim = image_feats.shape
    head_count = rel_bias.shape[0]
    heads_dim = w_proj.shape[0]
    head_size = heads_dim // head_count
    half_win = WIN // 2
    bias_span = rel_bias.shape[1]
    image_height = row_count * lax.axis_size("row")
    image_width = col_count * lax.axis_size("col")
    row_anchor = lax.axis_index("row") * row_count
    col_anchor = lax.axis_index("col") * col_count
    feats_f32 = image_feats.astype(jnp.float32)
    center = jnp.mean(feats_f32, axis=-1, keepdims=True)
    deviation = feats_f32 - center
    spread = jnp.mean(deviation * deviation, axis=-1, keepdims=True)
    inv_std = lax.rsqrt(spread + norm_eps)
    normal_x = deviation * inv_std
    normed = (normal_x * norm_gain).astype(jnp.bfloat16)
    normed_rows = normed.reshape(-1, model_dim)
    qkv_out = jnp.dot(normed_rows, w_qkv, preferred_element_type=jnp.float32).astype(jnp.bfloat16)
    qkv_out = qkv_out.reshape(tile_count, row_count, col_count, 3 * heads_dim)
    patch_count = row_count * col_count
    queries = qkv_out[..., :heads_dim].reshape(tile_count, patch_count, head_count, head_size)
    keys_values = qkv_out[..., heads_dim:]
    padded = with_halo(keys_values, (("row", 1), ("col", 2)), half_win)
    pad_rows = row_count + 2 * half_win
    pad_cols = col_count + 2 * half_win
    key_count = pad_rows * pad_cols
    flat_pad = padded.reshape(tile_count, key_count, 2 * heads_dim)
    pad_keys = flat_pad[..., :heads_dim].reshape(tile_count, key_count, head_count, head_size)
    pad_values = flat_pad[..., heads_dim:].reshape(tile_count, key_count, head_count, head_size)
    row_first = window_start(image_height, row_count, row_anchor) - (row_anchor - half_win)
    col_first = window_start(image_width, col_count, col_anchor) - (col_anchor - half_win)
    pad_row_pos = jnp.arange(pad_rows, dtype=jnp.int32)
    pad_col_pos = jnp.arange(pad_cols, dtype=jnp.int32)
    row_valid = (pad_row_pos[None, :] >= row_first[:, None]) & (
        pad_row_pos[None, :] < row_first[:, None] + WIN
    )
    col_valid = (pad_col_pos[None, :] >= col_first[:, None]) & (
        pad_col_pos[None, :] < col_first[:, None] + WIN
    )
    window_mask = (row_valid[:, None, :, None] & col_valid[None, :, None, :]).reshape(
        patch_count, key_count
    )
    bias_index = jnp.arange(bias_span, dtype=jnp.int32)
    rel_rows = pad_row_pos[None, :] - jnp.arange(row_count, dtype=jnp.int32)[:, None] + half_win
    rel_cols = pad_col_pos[None, :] - jnp.arange(col_count, dtype=jnp.int32)[:, None] + half_win
    row_onehot = (rel_rows[:, :, None] == bias_index[None, None, :]).astype(jnp.float32)
    col_onehot = (rel_cols[:, :, None] == bias_index[None, None, :]).astype(jnp.float32)
    bias_full = jnp.einsum(
        "rkx,hxy,cmy->hrckm", row_onehot, rel_bias, col_onehot, precision=highest
    )
    bias_full = bias_full.reshape(head_count, patch_count, key_count)
    score_scale = head_size ** (-0.5)
    scores = (
        jnp.einsum("bphd,bkhd->bhpk", queries, pad_keys, preferred_element_type=jnp.float32)
        * score_scale
        + bias_full[None]
    )
    scores = jnp.where(window_mask[None, None], scores, -1e30)
    row_peak = jnp.max(scores, axis=-1, keepdims=True)
    exp_terms = jnp.where(window_mask[None, None], jnp.exp(scores - row_peak), 0.0)
    probs_full = exp_terms / jnp.sum(exp_terms, axis=-1, keepdims=True)
    probs_low = probs_full.astype(jnp.bfloat16)
    attended = jnp.einsum(
        "bhpk,bkhd->bphd", probs_low, pad_values, preferred_element_type=jnp.float32
    ).astype(jnp.bfloat16)
    attended_rows = attended.reshape(-1, heads_dim)
    grad_rows = out_grad.reshape(-1, model_dim)
    layer_out = (
        feats_f32
        + jnp.dot(attended_rows, w_proj, preferred_element_type=jnp.float32).reshape(
            feats_f32.shape
        )
    ).astype(jnp.bfloat16)
    attended_grad = jnp.einsum(
        "td,ed->te", grad_rows, w_proj, preferred_element_type=jnp.float32
    ).astype(jnp.bfloat16)
    attn_grad = attended_grad.reshape(tile_count, patch_count, head_count, head_size)
    proj_part = jnp.einsum(
        "te,td->ed", attended_rows, grad_rows, preferred_element_type=jnp.float32
    )
    probs_grad = jnp.einsum(
        "bphd,bkhd->bhpk", attn_grad, pad_values, preferred_element_type=jnp.float32
    )
    inner_sum = jnp.sum(probs_full * probs_grad, axis=-1, keepdims=True)
    score_grad = probs_full * (probs_grad - inner_sum)
    block_grad = jnp.sum(score_grad, axis=0).reshape(
        head_count, row_count, col_count, pad_rows, pad_cols
    )
    score_low = score_grad.astype(jnp.bfloat16)
    query_grad = (
        jnp.einsum("bhpk,bkhd->bphd", score_low, pad_keys, preferred_element_type=jnp.float32)
        * score_scale
    ).astype(jnp.bfloat16)
    query_grad = query_grad.reshape(-1, heads_dim)
    key_pad_grad = (
        jnp.einsum("bhpk,bphd->bkhd", score_low, queries, preferred_element_type=jnp.float32)
        * score_scale
    )
    value_pad_grad = jnp.einsum(
        "bhpk,bphd->bkhd", probs_low, attn_grad, preferred_element_type=jnp.float32
    )
    kv_pad_grad = jnp.concatenate(
        [
            key_pad_grad.reshape(tile_count, key_count, heads_dim),
            value_pad_grad.reshape(tile_count, key_count, heads_dim),
        ],
        axis=-1,
    )
    kv_pad_grad = kv_pad_grad.reshape(tile_count, pad_rows, pad_cols, 2 * heads_dim)
    kv_grad = return_rims(kv_pad_grad, half_win)
    qkv_grad_rows = jnp.concatenate(
        [query_grad, kv_grad.astype(jnp.bfloat16).reshape(-1, 2 * heads_dim)], axis=-1
    )
    qkv_part = jnp.einsum(
        "td,te->de", normed_rows, qkv_grad_rows, preferred_element_type=jnp.float32
    )
    normed_grad = jnp.einsum(
        "te,de->td", qkv_grad_rows, w_qkv, preferred_element_type=jnp.float32
    ).reshape(feats_f32.shape)
    gain_part = jnp.sum(normed_grad * normal_x, axis=(0, 1, 2))
    bias_part = jnp.einsum(
        "rkx,hrckm,cmy->hxy", row_onehot, block_grad, col_onehot, precision=highest
    )
    flat_grads = jnp.concatenate([qkv_part.reshape(-1), proj_part.reshape(-1)])
    grad_share = lax.psum_scatter(flat_grads, ("row", "col"), scatter_dimension=0, tiled=True)
    summed = lax.all_gather(grad_share.astype(jnp.bfloat16), ("row", "col"), axis=0, tiled=True)
    qkv_length = qkv_part.shape[0] * qkv_part.shape[1]
    qkv_grad = summed[:qkv_length].reshape(qkv_part.shape)
    proj_grad = summed[qkv_length:].reshape(proj_part.shape)
    gain_grad, bias_grad = lax.psum((gain_part, bias_part), ("row", "col"))
    scaled = normed_grad * norm_gain
    correction = (
        scaled
        - jnp.mean(scaled, axis=-1, keepdims=True)
        - normal_x * jnp.mean(scaled * normal_x, axis=-1, keepdims=True)
    )
    feats_grad = (out_grad.astype(jnp.float32) + inv_std * correction).astype(jnp.bfloat16)
    return (layer_out, feats_grad, qkv_grad, proj_grad, gain_grad, bias_grad)


def solution(mesh):
    placed = (P(None, "row", "col", None), P(), P(), P(), P(), P(None, "row", "col", None))
    return jax.shard_map(
        body,
        mesh=mesh,
        in_specs=placed,
        out_specs=(P(None, "row", "col", None), P(None, "row", "col", None), P(), P(), P(), P()),
        check_vma=False,
    )
```

profile of v0, /device:TPU:32, one launch (start us, length us, event | category | flops | bytes accessed | tf_op | source)
XLA Modules:
  0.0 768.8 jit_solution(14767202913025241043)
XLA Ops:
  17.9 3.4 collective-permute-start
  21.3 4.6 collective-permute-start.1
  44.2 3.2 convolution_bitcast_fusion
  47.3 3.6 reshape.397
  50.9 3.0 pad_maximum_fusion.1
  66.2 5.2 fusion.14
  71.3 5.6 convolution_bitcast_fusion.2
  83.3 2.9 copy.43
  86.2 2.8 concatenate.31
  89.0 2.9 copy.41
  91.9 2.8 concatenate.30
  111.7 3.7 collective-permute-start.4
  117.7 3.6 reshape.398
  121.3 3.3 fusion.10
  128.0 3.5 collective-permute-start.6
  135.6 3.4 scatter-add.16
  146.4 3.1 multiply_reduce_fusion.1
  149.5 3.7 fusion.63
  156.8 6.9 reshape.385
  163.7 6.2 pad_maximum_fusion
  170.0 163.0 %all-reduce.3 = (bf16[2097152]{0:T(1024)(128)(2,1)}, f32[1024]{0:T(1024)}, f32[8,13,13]{2,1,0:T(8,128)}) all-reduce(f32[2097152]{0:T(1024)} %pad_maximum_fusion, f32[1024]{0:T(1024)S(1)} %get-tuple-element.72, f32[8,13,13]{2,1,0:T(8,128)} %convolution_bitcast_fusion.4), channel_id=2, replica_groups=mesh['row'=8,'col'=32] {'row','col'}, use_global_device_ids=true, to_apply=%region_7.8.clone | all-reduce | flops 2099528 | bytes 12601920
  342.4 405.0 %all-gather.2.cloned.1.call-done = bf16[2097152]{0:T(1024)(128)(2,1)} async-done(((bf16[8192]{0:T(1024)(128)(2,1)}), bf16[2097152]{0:T(1024)(128)(2,1)}) %all-gather.2.cloned.1.call-update) | async-done | bytes 4194320 | tf_op jit(solution)/shard_map/all_gather | solution.py:180
  747.4 3.2 slice.221
  750.6 6.8 reshape.388
  (113 shorter events, 99.2 us)
Async XLA Ops:
  7.2 5.6 copy-start
  7.2 740.3 %all-gather.2.cloned.1.call-start = ((), (), s32[]{:S(2)}) async-start(), calls=%async_computation | async-start | bytes 4210688 | tf_op jit(solution)/shard_map/all_gather | solution.py:180
  17.9 20.7 %collective-permute-start = (bf16[3,3,7,1024]{3,2,1,0:T(8,128)(2,1)}, bf16[3,3,7,1024]{3,2,1,0:T(8,128)(2,1)}, u32[]{:S(2)}, u32[]{:S(2)}) collective-permute-start(bf16[3,3,7,1024]{3,2,1,0:T(8,128)(2,1)} %get-tuple-element.91), channel_id=1, source_target_pairs={{0,32},{32,64},{64,96},{96,128},{128,160},{160,192},{192,224},{1,3... | collective-permute-start | bytes 387080 | tf_op jit(solution)/shard_map/ppermute | solution.py:22
  21.3 17.3 %collective-permute-start.1 = (bf16[3,3,7,1024]{3,2,1,0:T(8,128)(2,1)}, bf16[3,3,7,1024]{3,2,1,0:T(8,128)(2,1)}, u32[]{:S(2)}, u32[]{:S(2)}) collective-permute-start(bf16[3,3,7,1024]{3,2,1,0:T(8,128)(2,1)} %get-tuple-element.92), channel_id=1, source_target_pairs={{32,0},{64,32},{96,64},{128,96},{160,128},{192,160},{224,192},{33,... | collective-permute-start | bytes 387080 | tf_op jit(solution)/shard_map/ppermute | solution.py:25
  27.7 3.4 copy-start.8
  40.9 10.0 %collective-permute-start.2 = (bf16[3,13,3,1024]{3,2,1,0:T(4,128)(2,1)}, bf16[3,13,3,1024]{3,2,1,0:T(4,128)(2,1)}, u32[]{:S(2)}, u32[]{:S(2)}) collective-permute-start(bf16[3,13,3,1024]{3,2,1,0:T(4,128)(2,1)} %get-tuple-element.89), channel_id=1, source_target_pairs={{0,1},{1,2},{2,3},{3,4},{4,5},{5,6},{6,7},{7,8},{8,9},{9,10},{10,1... | collective-permute-start | bytes 718856 | tf_op jit(solution)/shard_map/ppermute | solution.py:22
  42.9 8.0 %collective-permute-start.3 = (bf16[3,13,3,1024]{3,2,1,0:T(4,128)(2,1)}, bf16[3,13,3,1024]{3,2,1,0:T(4,128)(2,1)}, u32[]{:S(2)}, u32[]{:S(2)}) collective-permute-start(bf16[3,13,3,1024]{3,2,1,0:T(4,128)(2,1)} %get-tuple-element.90), channel_id=1, source_target_pairs={{1,0},{2,1},{3,2},{4,3},{5,4},{6,5},{7,6},{8,7},{9,8},{10,9},{11,1... | collective-permute-start | bytes 718856 | tf_op jit(solution)/shard_map/ppermute | solution.py:25
  64.6 1.5 copy-start.5
  77.0 2.4 copy-start.6
  79.4 1.2 copy-start.4
  80.6 1.1 copy-start.9
  94.7 1.7 copy-start.7
  96.4 1.9 copy-start.2
  98.3 1.2 copy-start.13
  105.8 9.7 %copy-start.10 = (bf16[147,1024]{1,0:T(8,128)(2,1)S(1)}, bf16[147,1024]{1,0:T(8,128)(2,1)}, u32[]{:S(2)}) copy-start(bf16[147,1024]{1,0:T(8,128)(2,1)} %reshape.380) | copy-start | bytes 903172
  105.8 9.7 %copy-start.12 = (bf16[147,512]{1,0:T(8,128)(2,1)S(1)}, bf16[147,512]{1,0:T(8,128)(2,1)}, u32[]{:S(2)}) copy-start(bf16[147,512]{1,0:T(8,128)(2,1)} %reshape.386) | copy-start | bytes 451588
  109.3 16.6 %collective-permute-start.5 = (bf16[3,3,13,1024]{3,2,1,0:T(8,128)(2,1)}, bf16[3,3,13,1024]{3,2,1,0:T(8,128)(2,1)}, u32[]{:S(2)}, u32[]{:S(2)}) collective-permute-start(bf16[3,3,13,1024]{3,2,1,0:T(8,128)(2,1)} %get-tuple-element.83), channel_id=1, source_target_pairs={{32,0},{64,32},{96,64},{128,96},{160,128},{192,160},{224,192},{33,... | collective-permute-start | bytes 718856 | tf_op jit(solution)/shard_map/ppermute | solution.py:14
  111.7 13.1 %collective-permute-start.4 = (bf16[3,3,13,1024]{3,2,1,0:T(8,128)(2,1)}, bf16[3,3,13,1024]{3,2,1,0:T(8,128)(2,1)}, u32[]{:S(2)}, u32[]{:S(2)}) collective-permute-start(bf16[3,3,13,1024]{3,2,1,0:T(8,128)(2,1)} %get-tuple-element.84), channel_id=1, source_target_pairs={{0,32},{32,64},{64,96},{96,128},{128,160},{160,192},{192,224},{1,3... | collective-permute-start | bytes 718856 | tf_op jit(solution)/shard_map/ppermute | solution.py:14
  121.3 3.5 copy-start.1
  128.0 6.7 collective-permute-start.6
  133.4 5.6 collective-permute-start.7
  139.0 7.4 copy-start.14
  146.4 3.1 copy-start.11
  153.2 2.1 copy-start.3
Sparse Core Ops, SparseCore 0:
  334.4 413.0 all-gather.1
where the time goes:
time: 771 us; the launch traced here: 769 us
  waiting for transfers between devices  405 us (53%)
  blocking collectives  163 us (21%)
  local copies, waits for them, and re-layouts  93.5 us (12%)
  matrix products  39.9 us (5%)
  other arithmetic  31 us (4%)
  starting transfers between devices  22.1 us (3%)
  between operations  14.3 us (2%)
    all_gather x1, waiting for transfers between devices, body(): lax.all_gather(grad_share.astype(jnp.bfloat16), ('row', 'col'), axis=0, t...  405 us
    unnamed x1, blocking collectives  163 us
  transfers between devices with their start and end apart: 9, of which 2 were waited for; matrix products, arithmetic and copies ran while one was open for 6% of the time, Pallas kernels for 0%

commit v1 on v0

--- a/solution.py
+++ b/solution.py
@@ -177,7 +177,15 @@
     )
     flat_grads = jnp.concatenate([qkv_part.reshape(-1), proj_part.reshape(-1)])
     grad_share = lax.psum_scatter(flat_grads, ("row", "col"), scatter_dimension=0, tiled=True)
-    summed = lax.all_gather(grad_share.astype(jnp.bfloat16), ("row", "col"), axis=0, tiled=True)
+    summed = jnp.concatenate(
+        lax.all_to_all(
+            jnp.stack([grad_share.astype(jnp.bfloat16)] * lax.axis_size(("row", "col"))),
+            ("row", "col"),
+            0,
+            0,
+        ),
+        axis=0,
+    )
     qkv_length = qkv_part.shape[0] * qkv_part.shape[1]
     qkv_grad = summed[:qkv_length].reshape(qkv_part.shape)
     proj_grad = summed[qkv_length:].reshape(proj_part.shape)

time: 771 us -> 545 us (0.71)
  waiting for transfers between devices: 405 us -> 92.7 us
  local copies, waits for them, and re-layouts: 93.5 us -> 155 us
  other arithmetic: 31 us -> 56.4 us
  between operations: 14.3 us -> 1.2 us
  starting transfers between devices: 22.1 us -> 30.8 us
    all_gather x1 -> x0, waiting for transfers between devices: 405 us -> none  [body(): lax.all_gather(grad_share.astype(jnp.bfloat16), ('row', 'col'), axis=0, t...]
    all_to_all x0 -> x1, waiting for transfers between devices: none -> 92.7 us  [body(): lax.all_to_all(jnp.stack([grad_share.astype(jnp.bfloat16)] * lax.axis_siz...]
    unnamed x37 -> x51, local copies, waits for them, and re-layouts: 12.9 us -> 46.7 us
    another operation x2 -> x3, other arithmetic: 1.51 us -> 28.4 us  [the longest x1 26.9 us: body(): jnp.stack([grad_share.astype(jnp.bfloat16)] * lax.axis_size(('row', 'col')))]
    slice x1, local copies, waits for them, and re-layouts: 3.19 us -> 21.3 us  [body(): qkv_grad = summed[:qkv_length].reshape(qkv_part.shape)]
    all_to_all x0 -> x1, starting transfers between devices: none -> 8.75 us  [body(): lax.all_to_all(jnp.stack([grad_share.astype(jnp.bfloat16)] * lax.axis_siz...]
  transfers between devices with their start and end apart: 9 -> 9, of which waited for: 2 -> 2; matrix products, arithmetic and copies ran while one was open for 6% -> 7% of each run, Pallas kernels for 0% -> 0%
where the time goes in v1:
time: 545 us; the launch traced here: 536 us
  blocking collectives  162 us (30%)
  local copies, waits for them, and re-layouts  155 us (28%)
  waiting for transfers between devices  92.7 us (17%)
  other arithmetic  56.4 us (10%)
  matrix products  37.9 us (7%)
  starting transfers between devices  30.8 us (6%)
    unnamed x1, blocking collectives  162 us
    all_to_all x1, waiting for transfers between devices, body(): lax.all_to_all(jnp.stack([grad_share.astype(jnp.bfloat16)] * lax.axis_siz...  92.7 us
    unnamed x51, local copies, waits for them, and re-layouts  46.7 us
    another operation x1, other arithmetic, body(): jnp.stack([grad_share.astype(jnp.bfloat16)] * lax.axis_size(('row', 'col')))  26.9 us
    slice x1, local copies, waits for them, and re-layouts, body(): qkv_grad = summed[:qkv_length].reshape(qkv_part.shape)  21.3 us
  transfers between devices with their start and end apart: 9, of which 2 were waited for; matrix products, arithmetic and copies ran while one was open for 7% of the time, Pallas kernels for 0%

profile of v1, /device:TPU:32, one launch (start us, length us, event | category | flops | bytes accessed | tf_op | source)
XLA Modules:
  0.0 536.3 jit_solution(17094045198356224967)
XLA Ops:
  11.3 3.4 collective-permute-start
  14.7 4.6 collective-permute-start.1
  37.6 3.2 convolution_bitcast_fusion
  40.8 4.0 reshape.408
  60.1 5.2 fusion.9
  65.3 5.6 %convolution_bitcast_fusion.2 = f32[3,169,8,64]{1,3,2,0:T(8,128)} fusion(bf16[3,49,8,64]{3,2,1,0:T(8,128)(2,1)} %reshape.391, f32[3,8,49]{2,1,0:T(8,128)S(1)} %get-tuple-element.99, f32[3,8,49,169]{3,2,1,0:T(8,128)} %copy-done.7, pred[49,169]{1,0:T(8,128)(4,1)S(1)} %and.53), kind=kOutput, calls=%fused_computation.9 | convolution fusion | flops 26235552 | bytes 1996825 | tf_op jit(solution)/shard_map/bhpk,bphd->bkhd/dot_general | solution.py:153
  105.4 3.8 collective-permute-start.4
  111.5 3.6 reshape.409
  115.1 3.3 convolution_bitcast_fusion.3
  121.8 3.5 collective-permute-start.6
  128.8 3.4 scatter-add.16
  142.7 3.7 fusion.57
  147.8 7.1 %reshape.395 = f32[1572864]{0:T(1024)} reshape(f32[1024,1536]{1,0:T(8,128)} %fusion.57) | data formatting | bytes 12582912 | tf_op jit(solution)/shard_map/reshape | solution.py:178
  154.9 7.1 %pad_maximum_fusion = f32[2097152]{0:T(1024)} fusion(f32[524288]{0:T(1024)S(1)} %bitcast.82, f32[1572864]{0:T(1024)} %reshape.395), kind=kLoop, calls=%fused_computation.1 | loop fusion | flops 2097152 | bytes 16777216 | tf_op jit(solution)/shard_map/concatenate | solution.py:178
  162.1 162.2 %all-reduce.3 = (bf16[2097152]{0:T(1024)(128)(2,1)}, f32[1024]{0:T(1024)}, f32[8,13,13]{2,1,0:T(8,128)S(1)}) all-reduce(f32[2097152]{0:T(1024)} %pad_maximum_fusion, f32[1024]{0:T(1024)S(1)} %get-tuple-element.78, f32[8,13,13]{2,1,0:T(8,128)S(1)} %convolution_bitcast_fusion.5), channel_id=2, replica_groups=mesh['row'=8,'col'=32] {'row','col'}, use_global_device_ids=true, to_apply=%region_7.8.clone | all-reduce | flops 2099528 | bytes 12601920
  325.0 5.5 %stack.2 = bf16[256,1,8192]{2,1,0:T(2,128)(2,1)} broadcast(bf16[8192]{0:T(1024)(128)(2,1)S(1)} %dynamic-slice.34), dimensions={2} | broadcast | bytes 4210688 | tf_op jit(solution)/shard_map/stack | solution.py:182
  331.0 26.9 %reduce.13 = bf16[256,8192]{1,0:T(8,128)(2,1)} reduce(bf16[256,1,8192]{2,1,0:T(2,128)(2,1)} %stack.2, bf16[]{:T(256)} %broadcast.297), dimensions={1}, to_apply=%stack.2.reduce_sub_computation | reduce | bytes 8388610 | tf_op jit(solution)/shard_map/stack | solution.py:182
  357.9 7.8 %reshape.412 = bf16[256,2,4096]{2,1,0:T(2,128)(2,1)} reshape(bf16[256,8192]{1,0:T(8,128)(2,1)} %reduce.13) | data formatting | bytes 8388608
  365.7 8.7 %all-to-all-start = ((bf16[256,2,4096]{2,1,0:T(2,128)(2,1)}), bf16[256,2,4096]{2,1,0:T(2,128)(2,1)}, u32[]{:S(2)}, u32[]{:S(2)}) async-start(bf16[256,2,4096]{2,1,0:T(2,128)(2,1)} %reshape.412), calls=%async_computation | async-start | bytes 8388608 | tf_op jit(solution)/shard_map/all_to_all | solution.py:181
  377.7 92.7 %all-to-all-done = bf16[256,2,4096]{2,1,0:T(2,128)(2,1)} async-done(((bf16[256,2,4096]{2,1,0:T(2,128)(2,1)}), bf16[256,2,4096]{2,1,0:T(2,128)(2,1)}, u32[]{:S(2)}, u32[]{:S(2)}) %all-to-all-start) | async-done | bytes 4194336 | tf_op jit(solution)/shard_map/all_to_all | solution.py:181
  470.3 26.6 %reshape.413 = bf16[256,1,8192]{2,1,0:T(2,128)(2,1)} reshape(bf16[256,2,4096]{2,1,0:T(2,128)(2,1)} %all-to-all-done) | data formatting | bytes 8388608
  496.9 8.9 %slice_reduce_fusion.1 = bf16[64,8192]{1,0:T(8,128)(2,1)} fusion(bf16[256,1,8192]{2,1,0:T(2,128)(2,1)} %reshape.413), kind=kLoop, calls=%fused_computation.4 | loop fusion | bytes 2097152 | tf_op jit(solution)/shard_map/slice | solution.py:191
  505.8 21.3 %slice_reduce_fusion = bf16[192,8192]{1,0:T(8,128)(2,1)} fusion(bf16[256,1,8192]{2,1,0:T(2,128)(2,1)} %reshape.413), kind=kLoop, calls=%fused_computation.2 | loop fusion | bytes 6291456 | tf_op jit(solution)/shard_map/slice | solution.py:190
  527.1 6.7 %reshape.398 = bf16[1024,1536]{1,0:T(8,128)(2,1)} reshape(bf16[192,8192]{1,0:T(8,128)(2,1)} %slice_reduce_fusion) | data formatting | bytes 6291456 | tf_op jit(solution)/shard_map/reshape | solution.py:190
  (129 shorter events, 106.4 us)
Async XLA Ops:
  0.6 5.6 %copy-start = (bf16[1024,1536]{1,0:T(8,128)(2,1)S(1)}, bf16[1024,1536]{1,0:T(8,128)(2,1)}, u32[]{:S(2)}) copy-start(bf16[1024,1536]{1,0:T(8,128)(2,1)} %param.16) | copy-start | bytes 9437188
  11.3 20.7 %collective-permute-start = (bf16[3,3,7,1024]{3,2,1,0:T(8,128)(2,1)}, bf16[3,3,7,1024]{3,2,1,0:T(8,128)(2,1)}, u32[]{:S(2)}, u32[]{:S(2)}) collective-permute-start(bf16[3,3,7,1024]{3,2,1,0:T(8,128)(2,1)} %get-tuple-element.97), channel_id=1, source_target_pairs={{0,32},{32,64},{64,96},{96,128},{128,160},{160,192},{192,224},{1,3... | collective-permute-start | bytes 387080 | tf_op jit(solution)/shard_map/ppermute | solution.py:22
  14.7 17.3 %collective-permute-start.1 = (bf16[3,3,7,1024]{3,2,1,0:T(8,128)(2,1)}, bf16[3,3,7,1024]{3,2,1,0:T(8,128)(2,1)}, u32[]{:S(2)}, u32[]{:S(2)}) collective-permute-start(bf16[3,3,7,1024]{3,2,1,0:T(8,128)(2,1)} %get-tuple-element.98), channel_id=1, source_target_pairs={{32,0},{64,32},{96,64},{128,96},{160,128},{192,160},{224,192},{33,... | collective-permute-start | bytes 387080 | tf_op jit(solution)/shard_map/ppermute | solution.py:25
  21.1 3.4 copy-start.11
  34.3 10.5 %collective-permute-start.2 = (bf16[3,13,3,1024]{3,2,1,0:T(4,128)(2,1)}, bf16[3,13,3,1024]{3,2,1,0:T(4,128)(2,1)}, u32[]{:S(2)}, u32[]{:S(2)}) collective-permute-start(bf16[3,13,3,1024]{3,2,1,0:T(4,128)(2,1)} %get-tuple-element.95), channel_id=1, source_target_pairs={{0,1},{1,2},{2,3},{3,4},{4,5},{5,6},{6,7},{7,8},{8,9},{9,10},{10,1... | collective-permute-start | bytes 718856 | tf_op jit(solution)/shard_map/ppermute | solution.py:22
  36.3 8.5 %collective-permute-start.3 = (bf16[3,13,3,1024]{3,2,1,0:T(4,128)(2,1)}, bf16[3,13,3,1024]{3,2,1,0:T(4,128)(2,1)}, u32[]{:S(2)}, u32[]{:S(2)}) collective-permute-start(bf16[3,13,3,1024]{3,2,1,0:T(4,128)(2,1)} %get-tuple-element.96), channel_id=1, source_target_pairs={{1,0},{2,1},{3,2},{4,3},{5,4},{6,5},{7,6},{8,7},{9,8},{10,9},{11,1... | collective-permute-start | bytes 718856 | tf_op jit(solution)/shard_map/ppermute | solution.py:25
  70.9 2.4 copy-start.8
  90.3 1.9 copy-start.3
  99.6 9.6 %copy-start.13 = (bf16[147,1024]{1,0:T(8,128)(2,1)S(1)}, bf16[147,1024]{1,0:T(8,128)(2,1)}, u32[]{:S(2)}) copy-start(bf16[147,1024]{1,0:T(8,128)(2,1)} %reshape.390) | copy-start | bytes 903172
  99.6 9.6 %copy-start.18 = (bf16[147,512]{1,0:T(8,128)(2,1)S(1)}, bf16[147,512]{1,0:T(8,128)(2,1)}, u32[]{:S(2)}) copy-start(bf16[147,512]{1,0:T(8,128)(2,1)} %reshape.396) | copy-start | bytes 451588
  103.2 16.6 %collective-permute-start.5 = (bf16[3,3,13,1024]{3,2,1,0:T(8,128)(2,1)}, bf16[3,3,13,1024]{3,2,1,0:T(8,128)(2,1)}, u32[]{:S(2)}, u32[]{:S(2)}) collective-permute-start(bf16[3,3,13,1024]{3,2,1,0:T(8,128)(2,1)} %get-tuple-element.89), channel_id=1, source_target_pairs={{32,0},{64,32},{96,64},{128,96},{160,128},{192,160},{224,192},{33,... | collective-permute-start | bytes 718856 | tf_op jit(solution)/shard_map/ppermute | solution.py:14
  105.4 13.1 %collective-permute-start.4 = (bf16[3,3,13,1024]{3,2,1,0:T(8,128)(2,1)}, bf16[3,3,13,1024]{3,2,1,0:T(8,128)(2,1)}, u32[]{:S(2)}, u32[]{:S(2)}) collective-permute-start(bf16[3,3,13,1024]{3,2,1,0:T(8,128)(2,1)} %get-tuple-element.90), channel_id=1, source_target_pairs={{0,32},{32,64},{64,96},{96,128},{128,160},{160,192},{192,224},{1,3... | collective-permute-start | bytes 718856 | tf_op jit(solution)/shard_map/ppermute | solution.py:14
  115.1 3.4 copy-start.2
  121.8 6.1 %collective-permute-start.6 = (bf16[3,7,3,1024]{3,2,1,0:T(4,128)(2,1)S(1)}, bf16[3,7,3,1024]{3,2,1,0:T(4,128)(2,1)S(1)}, u32[]{:S(2)}, u32[]{:S(2)}) collective-permute-start(bf16[3,7,3,1024]{3,2,1,0:T(4,128)(2,1)S(1)} %get-tuple-element.94), channel_id=1, source_target_pairs={{0,1},{1,2},{2,3},{3,4},{4,5},{5,6},{6,7},{7,8},{8,9},{9,10},{10,1... | collective-permute-start | bytes 387080 | tf_op jit(solution)/shard_map/ppermute | solution.py:14
  126.6 5.6 %collective-permute-start.7 = (bf16[3,7,3,1024]{3,2,1,0:T(4,128)(2,1)}, bf16[3,7,3,1024]{3,2,1,0:T(4,128)(2,1)}, u32[]{:S(2)}, u32[]{:S(2)}) collective-permute-start(bf16[3,7,3,1024]{3,2,1,0:T(4,128)(2,1)} %get-tuple-element.93), channel_id=1, source_target_pairs={{1,0},{2,1},{3,2},{4,3},{5,4},{6,5},{7,6},{8,7},{9,8},{10,9},{11,1... | collective-permute-start | bytes 387080 | tf_op jit(solution)/shard_map/ppermute | solution.py:14
  132.2 7.4 %copy-start.20 = (f32[1024]{0:T(1024)S(1)}, f32[1024]{0:T(1024)}, u32[]{:S(2)}) copy-start(f32[1024]{0:T(1024)} %param.15) | copy-start | bytes 12292
  139.6 3.1 copy-start.15
  142.7 3.7 copy-start.16
  147.8 7.1 %copy-start.5 = (f32[64,8,8,128]{3,1,2,0:T(8,128)S(1)}, f32[64,8,8,128]{3,1,2,0:T(8,128)}, u32[]{:S(2)}) copy-start(f32[64,8,8,128]{3,1,2,0:T(8,128)} %copy.87) | copy-start | bytes 6291460
  365.7 8.8 %copy-start.14 = (bf16[3,49,8,64]{3,2,1,0:T(8,128)(2,1)S(1)}, bf16[3,49,8,64]{3,2,1,0:T(8,128)(2,1)}, u32[]{:S(2)}) copy-start(bf16[3,49,8,64]{3,2,1,0:T(8,128)(2,1)} %copy.55) | copy-start | bytes 451588
  365.7 9.0 %copy-start.10 = (bf16[512,1024]{1,0:T(8,128)(2,1)S(1)}, bf16[512,1024]{1,0:T(8,128)(2,1)}, u32[]{:S(2)}) copy-start(bf16[512,1024]{1,0:T(8,128)(2,1)} %param.18) | copy-start | bytes 3145732
  365.7 104.6 %all-to-all-start = ((bf16[256,2,4096]{2,1,0:T(2,128)(2,1)}), bf16[256,2,4096]{2,1,0:T(2,128)(2,1)}, u32[]{:S(2)}, u32[]{:S(2)}) async-start(bf16[256,2,4096]{2,1,0:T(2,128)(2,1)} %reshape.412), calls=%async_computation | async-start | bytes 8388608 | tf_op jit(solution)/shard_map/all_to_all | solution.py:181
  374.5 2.1 copy-start.17
  527.1 9.0 %copy-start.1 = (bf16[1024,1536]{1,0:T(8,128)(2,1)S(1)}, bf16[1024,1536]{1,0:T(8,128)(2,1)}, u32[]{:S(2)}) copy-start(bf16[1024,1536]{1,0:T(8,128)(2,1)} %param.16) | copy-start | bytes 9437188
  (6 other events, 7.7 us)
